TPU v7x, 128 devices: a whole 4x4x4 slice. The times are simulated.
128 devices in a mesh: seq: 16 (over x, y_hi, core), tp: 8 (over z, y_lo).
Axes of the slice: x: 4, y: 4 (y_hi: 2, y_lo: 2; y = y_hi * 2 + y_lo), z: 4, core: 2. Of those that a mesh axis runs over, the one named last changes fastest.
Arguments:
- byte_ids: int32 [4096, 8], P('seq'), may hold values from 0 to 255
- global_out: bfloat16 [4096, 8192], P('seq', 'tp'), may hold values from -6 to 6
- global_in_grad: bfloat16 [4096, 8192], P('seq', 'tp'), may hold values from -6 to 6
- out_grad: bfloat16 [32768, 1024], P(('seq', 'tp')), may hold values from -6 to 6
- proj_weight: bfloat16 [1024, 1024], replicated, may hold values from -0.1875 to 0.1875
- emb_local: bfloat16 [256, 1024], replicated, may hold values from -6 to 6
- norm_gain: float32 [1024], replicated, may hold values from 0.1 to 1.9
- up_weight: bfloat16 [1024, 2048], replicated, may hold values from -0.1875 to 0.1875
- down_weight: bfloat16 [2048, 1024], replicated, may hold values from -0.125 to 0.125
Outputs:
- glob_out_grad: bfloat16 [4096, 8192], P('seq', 'tp')
- emb_global_grad: float32 [256, 1024], replicated
- emb_local_grad: float32 [256, 1024], replicated
- gain_grad: float32 [1024], replicated
- proj_grad: float32 [1024, 1024], P(None, ('seq', 'tp'))
- up_grad: float32 [1024, 2048], P(None, ('seq', 'tp'))
- down_grad: float32 [2048, 1024], P(('seq', 'tp'))
All inputs are finite; a program needn't handle non-finite values.
Results may differ from a plain program's by a relative error of at most 0.015.
Values may be sent and summed in bfloat16 or wider, within the bound.
A program may use at most 128 MiB of HBM per device.

v0:
```python
import jax
import jax.numpy as jnp
from jax import lax
from jax.sharding import PartitionSpec as P


def inner(left, right):
    return lax.dot_general(
        left, right, (((0,), (0,)), ((), ())), preferred_element_type=jnp.float32
    )


def outer(left, right):
    return lax.dot_general(
        left, right, (((1,), (1,)), ((), ())), preferred_element_type=jnp.float32
    )


def on_device(
    byte_ids,
    global_out,
    global_in_grad,
    out_grad,
    proj_weight,
    emb_local,
    norm_gain,
    up_weight,
    down_weight,
):
    tp_count = lax.axis_size("tp")
    tp_place = lax.axis_index("tp")
    patch = byte_ids.shape[1]
    slot = proj_weight.shape[0]
    vocab = emb_local.shape[0]
    local_patches = global_out.shape[0] // tp_count
    local_ids = lax.dynamic_slice_in_dim(byte_ids, tp_place * local_patches, local_patches, 0)
    local_out = lax.all_to_all(global_out, "tp", split_axis=0, concat_axis=1, tiled=True)
    slot_in = local_out.reshape(local_patches * patch, slot)
    first = jnp.full((local_patches, 1), -1, jnp.int32)
    prev_id = jnp.concatenate([first, local_ids[:, :-1]], axis=1).reshape(-1)
    prev_hot = jax.nn.one_hot(prev_id, vocab, dtype=jnp.bfloat16)
    u_rows = jnp.dot(slot_in, proj_weight, preferred_element_type=jnp.float32) + jnp.dot(
        prev_hot, emb_local, preferred_element_type=jnp.float32
    )
    scale = lax.rsqrt(jnp.mean(u_rows * u_rows, axis=1, keepdims=True) + 1e-05)
    normed = u_rows * scale
    r_rows = (normed * norm_gain).astype(jnp.bfloat16)
    a_rows = jnp.dot(r_rows, up_weight, preferred_element_type=jnp.float32)
    sig = jax.nn.sigmoid(a_rows)
    h_rows = (a_rows * sig).astype(jnp.bfloat16)
    dh_rows = outer(out_grad, down_weight)
    da_rows = (dh_rows * sig * (1.0 + a_rows * (1.0 - sig))).astype(jnp.bfloat16)
    dr_rows = outer(da_rows, up_weight)
    dn_rows = dr_rows * norm_gain
    du_rows = (
        out_grad.astype(jnp.float32)
        + scale * (dn_rows - normed * jnp.mean(dn_rows * normed, axis=1, keepdims=True))
    ).astype(jnp.bfloat16)
    local_back = (
        outer(du_rows, proj_weight).astype(jnp.bfloat16).reshape(local_patches, patch * slot)
    )
    glob_out_grad = lax.all_to_all(local_back, "tp", split_axis=1, concat_axis=0, tiled=True)
    slots_here = patch // tp_count
    own_ids = lax.dynamic_slice_in_dim(byte_ids, tp_place * slots_here, slots_here, 1).reshape(-1)
    own_hot = jax.nn.one_hot(own_ids, vocab, dtype=jnp.bfloat16)
    emb_global_part = inner(own_hot, global_in_grad)
    emb_local_part = inner(prev_hot, du_rows)
    gain_part = jnp.sum(dr_rows * normed, axis=0)
    emb_global_grad, emb_local_grad, gain_grad = lax.psum(
        (emb_global_part, emb_local_part, gain_part), ("seq", "tp")
    )
    proj_part = inner(slot_in, du_rows)
    up_part = inner(r_rows, da_rows)
    down_part = inner(h_rows, out_grad)
    proj_grad, up_grad, down_grad = (
        lax.psum_scatter(proj_part, ("seq", "tp"), scatter_dimension=1, tiled=True),
        lax.psum_scatter(up_part, ("seq", "tp"), scatter_dimension=1, tiled=True),
        lax.psum_scatter(down_part, ("seq", "tp"), scatter_dimension=0, tiled=True),
    )
    return (
        glob_out_grad,
        emb_global_grad,
        emb_local_grad,
        gain_grad,
        proj_grad,
        up_grad,
        down_grad,
    )


def solution(mesh):
    placed = (
        P("seq", None),
        P("seq", "tp"),
        P("seq", "tp"),
        P(("seq", "tp"), None),
        P(),
        P(),
        P(),
        P(),
        P(),
    )
    return jax.shard_map(
        on_device,
        mesh=mesh,
        in_specs=placed,
        out_specs=(
            P("seq", "tp"),
            P(),
            P(),
            P(),
            P(None, ("seq", "tp")),
            P(None, ("seq", "tp")),
            P(("seq", "tp"), None),
        ),
        check_vma=False,
    )
```

profile of v0, /device:TPU:0, one launch (start us, length us, event | category | flops | bytes accessed | tf_op | source)
XLA Modules:
  0.0 2162.4 jit_solution(6053280185825184937)
XLA Ops:
  7.2 0.0 copy-start
  7.2 6.6 all-to-all-start
  13.8 0.0 all-reduce.4.cloned.1.call-start
  13.8 0.8 constant_dynamic-slice_fusion.1
  14.6 0.1 copy.25
  14.7 0.1 concatenate.3.clone
  14.7 0.1 eq.37
  14.8 0.7 constant_dynamic-slice_fusion
  15.5 2.4 fusion.11
  18.0 5.9 all-to-all-done
  23.8 0.0 copy-start.1
  23.8 0.0 copy-start.8
  23.8 0.8 copy-done.1
  24.6 0.0 copy-done
  24.6 0.0 copy-start.4
  24.6 0.8 fusion.6
  25.5 0.0 copy-done.8
  25.5 0.0 copy-start.11
  25.5 0.4 multiply_reduce_fusion.2
  25.9 0.9 copy-done.4
  26.9 0.0 copy-done.11
  26.9 0.0 copy-start.9
  26.9 0.0 copy-start.12
  26.9 1.3 fusion.17
  28.2 0.0 copy-done.9
  28.2 1.0 copy-done.12
  29.2 0.0 copy-start.5
  29.2 1.5 fusion.1
  30.8 0.0 copy-done.5
  30.8 0.0 copy-start.6
  30.8 1.5 multiply_reduce_fusion
  32.3 0.0 copy-done.6
  32.3 0.3 add_convert_fusion
  32.6 0.0 copy-start.2
  32.6 0.8 copy-done.2
  33.4 1.4 fusion.10
  34.8 0.0 all-reduce.4.cloned.1.call-update
  34.8 0.0 reduce-scatter.4.cloned.1.call-start
  34.9 4.0 convolution_bitcast_fusion
  38.9 0.0 reduce-scatter.4.cloned.1.call-update
  38.9 0.0 reduce-scatter.6.cloned.1.call-start
  39.0 5.8 fusion.16
  44.8 0.0 copy-start.10
  44.8 0.0 reduce-scatter.6.cloned.1.call-update
  44.8 0.0 reduce-scatter.8.cloned.1.call-start
  44.8 1.0 copy-done.10
  45.8 6.2 fusion.3
  52.0 0.0 copy-start.3
  52.0 0.0 reduce-scatter.8.cloned.1.call-update
  52.0 1.0 copy-done.3
  53.1 0.7 fusion.2
  53.8 1.1 copy.24
  54.9 3.5 all-to-all-start.1
  58.4 66.5 %psum.23 = f32[1024]{0:T(1024)} all-reduce(f32[1024]{0:T(1024)S(1)} %get-tuple-element.7), channel_id=1, replica_groups=mesh['seq'=16,'tp'=8] {'seq','tp'}, use_global_device_ids=true, to_apply=%region_5.6 | all-reduce | flops 1024 | bytes 8192 | tf_op jit(solution)/shard_map/psum | solution.py:69
  124.9 0.0 all-to-all-done.1
  124.9 62.7 %all-reduce.4.cloned.1.call-done = (f32[256,1024]{1,0:T(8,128)}, f32[256,1024]{1,0:T(8,128)}) async-done(((f32[256,1024]{1,0:T(8,128)}, f32[256,1024]{1,0:T(8,128)}), (f32[256,1024]{1,0:T(8,128)}, f32[256,1024]{1,0:T(8,128)})) %all-reduce.4.cloned.1.call-update) | async-done | bytes 2097168 | tf_op jit(solution)/shard_map/psum | solution.py:69
  187.7 651.5 %reduce-scatter.4.cloned.1.call-done = f32[1024,8]{0,1:T(8,128)} async-done(((f32[1024,1024]{0,1:T(8,128)}), f32[1024,8]{0,1:T(8,128)}) %reduce-scatter.4.cloned.1.call-update) | async-done | bytes 32784 | tf_op jit(solution)/shard_map/reduce_scatter | solution.py:76
  839.2 656.4 %reduce-scatter.6.cloned.1.call-done = f32[1024,16]{0,1:T(8,128)} async-done(((f32[1024,2048]{0,1:T(8,128)}), f32[1024,16]{0,1:T(8,128)}) %reduce-scatter.6.cloned.1.call-update) | async-done | bytes 65552 | tf_op jit(solution)/shard_map/reduce_scatter | solution.py:77
  1495.7 656.1 %reduce-scatter.8.cloned.1.call-done = f32[16,1024]{1,0:T(8,128)} async-done(((f32[2048,1024]{1,0:T(8,128)}), f32[16,1024]{1,0:T(8,128)}) %reduce-scatter.8.cloned.1.call-update) | async-done | bytes 65552 | tf_op jit(solution)/shard_map/reduce_scatter | solution.py:78
  2151.8 0.0 copy-start.7
  2151.8 0.8 copy.37
  2152.6 2.3 copy.38
  2154.9 0.0 copy-done.7
  2154.9 1.0 copy.39
  (2 shorter events, 0.0 us)
Async XLA Ops:
  7.2 17.5 copy-start
  7.2 16.7 all-to-all-start
  13.8 173.9 %all-reduce.4.cloned.1.call-start = ((), (), s32[]{:S(2)}) async-start(), calls=%async_computation.8 | async-start | bytes 4194304 | tf_op jit(solution)/shard_map/psum | solution.py:69
  23.8 0.8 copy-start.1
  23.8 1.6 copy-start.8
  24.6 2.2 copy-start.4
  25.5 1.4 copy-start.11
  26.9 1.3 copy-start.9
  26.9 2.4 copy-start.12
  29.2 1.6 copy-start.5
  30.8 1.5 copy-start.6
  32.6 0.8 copy-start.2
  34.8 804.4 %reduce-scatter.4.cloned.1.call-start = ((), (), s32[]{:S(2)}) async-start(), calls=%async_computation.5 | async-start | bytes 4227072 | tf_op jit(solution)/shard_map/reduce_scatter | solution.py:76
  38.9 1456.8 %reduce-scatter.6.cloned.1.call-start = ((), (), s32[]{:S(2)}) async-start(), calls=%async_computation.6 | async-start | bytes 8454144 | tf_op jit(solution)/shard_map/reduce_scatter | solution.py:77
  44.8 1.0 copy-start.10
  44.8 2107.0 %reduce-scatter.8.cloned.1.call-start = ((), (), s32[]{:S(2)}) async-start(), calls=%async_computation.7 | async-start | bytes 8454144 | tf_op jit(solution)/shard_map/reduce_scatter | solution.py:78
  52.0 1.0 copy-start.3
  54.9 70.0 %all-to-all-start.1 = ((bf16[32,8,1024]{2,0,1:T(8,128)(2,1)}), bf16[32,8,1024]{2,0,1:T(8,128)(2,1)S(1)}, u32[]{:S(2)}, u32[]{:S(2)}) async-start(bf16[32,8,1024]{2,0,1:T(8,128)(2,1)} %copy.24), calls=%async_computation.1 | async-start | bytes 1048576 | tf_op jit(solution)/shard_map/all_to_all | solution.py:62
  2151.8 3.1 copy-start.7
Sparse Core Ops, SparseCore 0:
  35.0 152.6 all-reduce.3
  190.6 648.5 reduce-scatter.3
  842.2 653.4 reduce-scatter.5
  1498.5 653.3 reduce-scatter.7
where the time goes:
time: 2160 us
  waiting for transfers between devices  2030 us (94%)
  blocking collectives  66.5 us (3%)
  matrix products  26.2 us (1%)
    reduce_scatter x1, waiting for transfers between devices, on_device(): lax.psum_scatter(up_part, ('seq', 'tp'), scatter_dimension=1, tiled=True)  656 us
    reduce_scatter x1, waiting for transfers between devices, on_device(): lax.psum_scatter(down_part, ('seq', 'tp'), scatter_dimension=0, tiled=True)  656 us
    reduce_scatter x1, waiting for transfers between devices, on_device(): lax.psum_scatter(proj_part, ('seq', 'tp'), scatter_dimension=1, tiled=True)  652 us
    psum x1, blocking collectives, on_device(): lax.psum((emb_global_part, emb_local_part, gain_part), ('seq', 'tp'))  66.5 us
    psum x1, waiting for transfers between devices, on_device(): lax.psum((emb_global_part, emb_local_part, gain_part), ('seq', 'tp'))  62.7 us
  transfers between devices with their start and end apart: 6, of which 5 were waited for; matrix products, arithmetic and copies ran while one was open for 1% of the time, Pallas kernels for 0%

commit v1 on v0

--- a/solution.py
+++ b/solution.py
@@ -2,6 +2,12 @@
 import jax.numpy as jnp
 from jax import lax
 from jax.sharding import PartitionSpec as P
+
+
+def set_reach(page):
+    for s in ("tp", "seq"):
+        page = lax.psum(page, s)
+    return page
 
 
 def inner(left, right):
@@ -66,8 +72,8 @@
     emb_global_part = inner(own_hot, global_in_grad)
     emb_local_part = inner(prev_hot, du_rows)
     gain_part = jnp.sum(dr_rows * normed, axis=0)
-    emb_global_grad, emb_local_grad, gain_grad = lax.psum(
-        (emb_global_part, emb_local_part, gain_part), ("seq", "tp")
+    emb_global_grad, emb_local_grad, gain_grad = set_reach(
+        (emb_global_part, emb_local_part, gain_part)
     )
     proj_part = inner(slot_in, du_rows)
     up_part = inner(r_rows, da_rows)

time: 2160 us -> 2120 us (0.981)
  waiting for transfers between devices: 2030 us -> 2000 us
    reduce_scatter x1, waiting for transfers between devices: 652 us -> 509 us  [on_device(): lax.psum_scatter(proj_part, ('seq', 'tp'), scatter_dimension=1, tiled=True)]
    psum x1 -> x2, waiting for transfers between devices: 62.7 us -> 169 us  [set_reach(): page = lax.psum(page, s)]
    psum x1 -> x2, blocking collectives: 66.5 us -> 59.2 us  [set_reach(): page = lax.psum(page, s)]
  transfers between devices with their start and end apart: 6 -> 7, of which waited for: 5 -> 6; matrix products, arithmetic and copies ran while one was open for 1% -> 1% of each run, Pallas kernels for 0% -> 0%
where the time goes in v1:
time: 2120 us
  waiting for transfers between devices  2000 us (94%)
  blocking collectives  59.2 us (3%)
  matrix products  26.2 us (1%)
    reduce_scatter x1, waiting for transfers between devices, on_device(): lax.psum_scatter(up_part, ('seq', 'tp'), scatter_dimension=1, tiled=True)  656 us
    reduce_scatter x1, waiting for transfers between devices, on_device(): lax.psum_scatter(down_part, ('seq', 'tp'), scatter_dimension=0, tiled=True)  656 us
    reduce_scatter x1, waiting for transfers between devices, on_device(): lax.psum_scatter(proj_part, ('seq', 'tp'), scatter_dimension=1, tiled=True)  509 us
    psum x2, waiting for transfers between devices, set_reach(): page = lax.psum(page, s)  169 us
    psum x2, blocking collectives, set_reach(): page = lax.psum(page, s)  59.2 us
  transfers between devices with their start and end apart: 7, of which 6 were waited for; matrix products, arithmetic and copies ran while one was open for 1% of the time, Pallas kernels for 0%

profile of v1, /device:TPU:0, one launch (start us, length us, event | category | flops | bytes accessed | tf_op | source)
XLA Modules:
  0.0 2119.5 jit_solution(14036991199184751554)
XLA Ops:
  8.0 0.0 copy-start
  8.0 6.6 all-to-all-start
  14.6 0.0 all-reduce.8.cloned.1.call-start
  14.6 0.8 constant_dynamic-slice_fusion.1
  15.4 0.1 copy.25
  15.5 0.1 concatenate.3.clone
  15.6 0.1 eq.37
  15.7 0.7 constant_dynamic-slice_fusion
  16.4 2.4 fusion.11
  18.8 5.9 all-to-all-done
  24.7 0.0 copy-start.1
  24.7 0.0 copy-start.8
  24.7 0.8 copy-done.1
  25.5 0.0 copy-done
  25.5 0.0 copy-start.4
  25.5 0.8 fusion.6
  26.3 0.0 copy-done.8
  26.3 0.0 copy-start.11
  26.3 0.4 multiply_reduce_fusion.2
  26.8 0.9 copy-done.4
  27.7 0.0 copy-done.11
  27.7 0.0 copy-start.9
  27.7 0.0 copy-start.12
  27.7 1.3 fusion.17
  29.0 0.0 copy-done.9
  29.0 1.0 copy-done.12
  30.1 1.5 fusion.1
  31.6 0.0 copy-done.5
  31.6 0.0 copy-start.6
  31.6 1.5 multiply_reduce_fusion
  33.1 0.0 copy-done.6
  33.1 0.3 add_convert_fusion
  33.5 0.0 copy-start.2
  33.5 0.8 copy-done.2
  34.3 1.4 fusion.10
  35.6 0.0 all-reduce.8.cloned.1.call-update
  35.7 0.0 all-reduce.6.cloned.1.call-start
  35.7 104.0 %all-reduce.8.cloned.1.call-done = (f32[256,1024]{1,0:T(8,128)}, f32[256,1024]{1,0:T(8,128)}) async-done(((f32[256,1024]{1,0:T(8,128)}, f32[256,1024]{1,0:T(8,128)}), (f32[256,1024]{1,0:T(8,128)}, f32[256,1024]{1,0:T(8,128)})) %all-reduce.8.cloned.1.call-update) | async-done | bytes 2097168 | tf_op jit(solution)/shard_map/psum | solution.py:9
  139.7 0.0 all-reduce.6.cloned.1.call-update
  139.8 0.0 reduce-scatter.4.cloned.1.call-start
  139.8 4.0 convolution_bitcast_fusion
  143.8 0.0 reduce-scatter.4.cloned.1.call-update
  143.8 0.0 reduce-scatter.6.cloned.1.call-start
  143.9 5.8 fusion.16
  149.7 0.0 reduce-scatter.6.cloned.1.call-update
  149.7 0.0 reduce-scatter.8.cloned.1.call-start
  149.8 1.0 copy-done.10
  150.7 6.2 fusion.3
  156.9 0.0 reduce-scatter.8.cloned.1.call-update
  157.0 1.0 copy-done.3
  158.0 0.7 fusion.2
  158.7 1.1 copy.24
  159.8 3.5 all-to-all-start.1
  163.3 25.3 %psum.46 = f32[1024]{0:T(1024)S(1)} all-reduce(f32[1024]{0:T(1024)S(1)} %get-tuple-element.7), channel_id=1, replica_groups=mesh['seq'=16,'tp'=8] {'tp'}, use_global_device_ids=true, to_apply=%region_7.8 | all-reduce | flops 1024 | bytes 8192 | tf_op jit(solution)/shard_map/psum | solution.py:9
  188.6 33.9 %psum.47 = f32[1024]{0:T(1024)} all-reduce(f32[1024]{0:T(1024)S(1)} %psum.46), channel_id=1, replica_groups=mesh['seq'=16,'tp'=8] {'seq'}, use_global_device_ids=true, to_apply=%region_8.9 | all-reduce | flops 1024 | bytes 8192 | tf_op jit(solution)/shard_map/psum | solution.py:9
  222.5 0.0 all-to-all-done.1
  222.5 64.8 %all-reduce.6.cloned.1.call-done = (f32[256,1024]{1,0:T(8,128)}, f32[256,1024]{1,0:T(8,128)}) async-done(((f32[256,1024]{1,0:T(8,128)}, f32[256,1024]{1,0:T(8,128)}), (f32[256,1024]{1,0:T(8,128)}, f32[256,1024]{1,0:T(8,128)})) %all-reduce.6.cloned.1.call-update) | async-done | bytes 2097168 | tf_op jit(solution)/shard_map/psum | solution.py:9
  287.3 508.8 %reduce-scatter.4.cloned.1.call-done = f32[1024,8]{0,1:T(8,128)} async-done(((f32[1024,1024]{0,1:T(8,128)}), f32[1024,8]{0,1:T(8,128)}) %reduce-scatter.4.cloned.1.call-update) | async-done | bytes 32784 | tf_op jit(solution)/shard_map/reduce_scatter | solution.py:82
  796.1 656.1 %reduce-scatter.6.cloned.1.call-done = f32[1024,16]{0,1:T(8,128)} async-done(((f32[1024,2048]{0,1:T(8,128)}), f32[1024,16]{0,1:T(8,128)}) %reduce-scatter.6.cloned.1.call-update) | async-done | bytes 65552 | tf_op jit(solution)/shard_map/reduce_scatter | solution.py:83
  1452.2 655.7 %reduce-scatter.8.cloned.1.call-done = f32[16,1024]{1,0:T(8,128)} async-done(((f32[2048,1024]{1,0:T(8,128)}), f32[16,1024]{1,0:T(8,128)}) %reduce-scatter.8.cloned.1.call-update) | async-done | bytes 65552 | tf_op jit(solution)/shard_map/reduce_scatter | solution.py:84
  2107.9 0.8 copy.39
  2108.7 2.3 copy.40
  2111.0 0.0 copy-done.7
  2111.0 1.0 copy.41
  (6 shorter events, 0.0 us)
Async XLA Ops:
  8.0 17.5 copy-start
  8.0 16.7 all-to-all-start
  14.6 125.1 %all-reduce.8.cloned.1.call-start = ((), (), s32[]{:S(2)}) async-start(), calls=%async_computation.9 | async-start | bytes 4194304 | tf_op jit(solution)/shard_map/psum | solution.py:9
  24.7 0.8 copy-start.1
  24.7 1.6 copy-start.8
  25.5 2.2 copy-start.4
  26.3 1.4 copy-start.11
  27.7 1.3 copy-start.9
  27.7 2.4 copy-start.12
  30.1 1.6 copy-start.5
  31.6 1.5 copy-start.6
  33.5 0.8 copy-start.2
  35.7 251.6 %all-reduce.6.cloned.1.call-start = ((), (), s32[]{:S(2)}) async-start(), calls=%async_computation.8 | async-start | bytes 4194304 | tf_op jit(solution)/shard_map/psum | solution.py:9
  139.8 656.3 %reduce-scatter.4.cloned.1.call-start = ((), (), s32[]{:S(2)}) async-start(), calls=%async_computation.5 | async-start | bytes 4227072 | tf_op jit(solution)/shard_map/reduce_scatter | solution.py:82
  143.8 1308.3 %reduce-scatter.6.cloned.1.call-start = ((), (), s32[]{:S(2)}) async-start(), calls=%async_computation.6 | async-start | bytes 8454144 | tf_op jit(solution)/shard_map/reduce_scatter | solution.py:83
  149.7 1.1 copy-start.10
  149.7 1958.2 %reduce-scatter.8.cloned.1.call-start = ((), (), s32[]{:S(2)}) async-start(), calls=%async_computation.7 | async-start | bytes 8454144 | tf_op jit(solution)/shard_map/reduce_scatter | solution.py:84
  156.9 1.0 copy-start.3
  159.8 62.7 %all-to-all-start.1 = ((bf16[32,8,1024]{2,0,1:T(8,128)(2,1)}), bf16[32,8,1024]{2,0,1:T(8,128)(2,1)S(1)}, u32[]{:S(2)}, u32[]{:S(2)}) async-start(bf16[32,8,1024]{2,0,1:T(8,128)(2,1)} %copy.24), calls=%async_computation.1 | async-start | bytes 1048576 | tf_op jit(solution)/shard_map/all_to_all | solution.py:68
  2107.9 3.1 copy-start.7
Sparse Core Ops, SparseCore 0:
  35.8 103.8 all-reduce.7
  142.3 144.9 all-reduce.5
Sparse Core Ops, SparseCore 1:
  143.9 652.1 reduce-scatter.3
  798.9 653.2 reduce-scatter.5
  1455.0 652.8 reduce-scatter.7
